TPU v7x, 32 devices: a whole 2x2x4 slice. The times are simulated.
32 devices in a mesh: prow: 4 (over z), pcol: 8 (over y, x, core).
Axes of the slice: x: 2, y: 2, z: 4, core: 2. Of those that a mesh axis runs over, the one named last changes fastest.
Arguments:
- matrix: float32 [6, 4, 256, 3, 8, 256], P(None, 'prow', None, None, 'pcol'), may hold values from -6 to 6
- row_order: int32 [6144], replicated, may hold values from 0 to 6143, as said below
- inverses: float32 [4, 256, 256], replicated, may hold values from -0.0234375 to 0.0234375
- lower_fill: int32 [4, 24], replicated, may hold values 0 or 1
- upper_fill: int32 [4, 24], replicated, may hold values 0 or 1
Outputs:
- factored: float32 [6, 4, 256, 3, 8, 256], P(None, 'prow', None, None, 'pcol')
Inputs may be any that keep to these rules, and one draw needn't show every extreme that they name: row_order is a permutation of the rows; of the rows whose block row index is congruent to p modulo the number of indices of prow, exactly 6 * 256 divided by that number go to rows whose block row index is congruent to s, for every p and s.
All inputs are finite; a program needn't handle non-finite values.
Results may differ from a plain program's by a relative error of at most 0.0002.
Values sent between devices are 32-bit elements; how exact they have to be, the bound alone decides.
A program may use at most 128 MiB of HBM per device.

v0:
```python
import functools

import jax
import jax.numpy as jnp
from jax import lax
from jax.experimental import pallas as pl
from jax.experimental.pallas import tpu as pltpu
from jax.sharding import PartitionSpec as P


def mm(a, b):
    return jnp.dot(a, b, precision=lax.Precision.HIGH, preferred_element_type=jnp.float32)


def index_lists(row_order, rows, width, prows, here_row):
    local_rows = rows * width
    blocks = row_order.reshape(rows, prows, width)
    targets = lax.dynamic_index_in_dim(blocks, here_row, 1, keepdims=False).reshape(-1)
    local = jnp.arange(local_rows, dtype=jnp.int32)
    sending = (targets // width % prows) * local_rows + local
    by_source = jnp.transpose(blocks, (1, 0, 2)).reshape(-1)
    dest_local = by_source // width // prows * width + by_source % width
    mine = by_source // width % prows == here_row
    position = jnp.cumsum(mine.astype(jnp.int32)) - 1
    key = jnp.where(mine, dest_local * local_rows + position, local_rows * local_rows)
    both = jnp.concatenate([sending, prows * local_rows + key])
    both = lax.sort(both, is_stable=False)[: 2 * local_rows] % local_rows
    return both[:local_rows], both[local_rows:]


def keep_of(fill_row, panel, blocks):
    return (blocks > panel) & (fill_row[blocks] == 1)


def body(matrix, row_order, inverses, lower_fill, upper_fill):
    nrows = matrix.shape[0]
    width = matrix.shape[2]
    ncols = matrix.shape[3]
    prows = lax.axis_size("prow")
    pcols = lax.axis_size("pcol")
    p = lax.axis_index("prow")
    q = lax.axis_index("pcol")
    panels = inverses.shape[0]
    local_rows = nrows * width
    cols = ncols * width
    sending, taking = index_lists(row_order, nrows, width, prows, p)
    work = matrix.reshape(local_rows, cols)
    outgoing = work[sending].reshape(prows, local_rows // prows, cols)
    incoming = lax.all_to_all(outgoing, "prow", split_axis=0, concat_axis=0, tiled=True)
    work = incoming.reshape(local_rows, cols)[taking]
    tops = lax.all_gather(work[:width], "prow", axis=0, tiled=False)[:panels]
    tops = tops.reshape(panels * width, cols)
    column = jnp.concatenate([tops[:, :width], work[:, :width]], axis=0)
    ratio = pcols // panels
    pieces = column.reshape(ratio, -1, width)
    piece = jnp.where(q < panels, pieces[0], 0.0)
    for j in range(1, ratio):
        pairs = [(k, k + panels * j) for k in range(panels)]
        piece = piece + lax.ppermute(pieces[j], "pcol", pairs)
    every = lax.all_gather(piece, "pcol", axis=0, tiled=False)
    every = every.reshape(ratio, panels, piece.shape[0], width)
    columns = [every[:, k].reshape(column.shape) for k in range(panels)]
    row_blocks = jnp.concatenate(
        [jnp.arange(panels, dtype=jnp.int32), jnp.arange(nrows, dtype=jnp.int32) * prows + p]
    )
    col_blocks = jnp.arange(ncols, dtype=jnp.int32) * pcols + q
    corner = panels * width
    lowers, uppers = [], []
    mine = work[:, :width]
    for k in range(panels):
        here = columns[k]
        for m in range(k):
            keep = (upper_fill[m, k] == 1).astype(jnp.float32)
            part = here[m * width : (m + 1) * width] * keep
            here = here - mm(lowers[m], part)
        columns[k] = here
        row_keep = jnp.repeat(keep_of(lower_fill[k], k, row_blocks), width)[:, None]
        lower = jnp.where(row_keep, mm(here, inverses[k]), 0.0)
        lowers.append(lower)
        row = tops[k * width : (k + 1) * width]
        for m in range(k):
            row = row - mm(lower_rows(lowers[m], k, width), uppers[m])
        col_keep = jnp.repeat(keep_of(upper_fill[k], k, col_blocks), width)[None, :]
        uppers.append(jnp.where(col_keep, row, 0.0))
    left = jnp.concatenate([x[corner:] for x in lowers], axis=1)
    out = work - mm(left, jnp.concatenate(uppers, axis=0))
    row_ids = jnp.repeat(row_blocks[panels:], width)[:, None]
    first = out[:, :width]
    for k in range(panels):
        first = jnp.where((q == k) & (row_ids > k), lowers[k][corner:], first)
    out = out.at[:, :width].set(first)
    return out.reshape(nrows, 1, width, ncols, 1, width)


def lower_rows(lower, k, width):
    return lower[k * width : (k + 1) * width]


MESH = pl.DeviceIdType.MESH


def exchange_kernel(
    nrows, width, sending, taking, mat, work, tops, cols,
    send, recv0, recv1, recv2, a2a_send, a2a_recv, ag_send, ag_recv, x_send, x_recv, y_send, y_recv,
    s_send, s_recv, local_sem,
):
    p = lax.axis_index("prow")
    q = lax.axis_index("pcol")
    side, across, core = q // 4, q // 2 % 2, q % 2
    xq = side * 4 + (1 - across) * 2 + core
    yq = (1 - side) * 4 + across * 2 + core
    sq = side * 4 + across * 2 + (1 - core)
    local_rows = nrows * width
    share = local_rows // 4
    top = 2 * width
    size = 4 * width
    others = [((p + t) % 4, q) for t in (2, 1, 3)]

    recv = (recv0, recv1, recv2)
    barrier = pltpu.get_barrier_semaphore()
    for peer in others + [(p, xq), (p, yq), (p, sq)]:
        pl.semaphore_signal(barrier, inc=1, device_id=peer, device_id_type=MESH)
    pl.semaphore_wait(barrier, 6)

    def remote(src, dst, send_sem, recv_sem, peer):
        return pltpu.make_async_remote_copy(
            src_ref=src, dst_ref=dst, send_sem=send_sem, recv_sem=recv_sem,
            device_id=peer, device_id_type=MESH,
        )

    def pick(dst, index, index_base, source, pitch, offset, count):
        unroll = 8

        def group(g, carry):
            for u in range(unroll):
                row = index[index_base + g * unroll + u]
                dst[pl.ds(g * (2 * unroll) + 2 * u, 2), :] = source[
                    pl.ds(row * pitch + offset, 2), :
                ]
            return carry

        lax.fori_loop(0, count // unroll, group, 0)

    def a2a(c, slot):
        peer = others[slot]
        here = recv[c].at[pl.ds(pl.multiple_of(p * (2 * share), 8), 2 * share)]
        return remote(send.at[c, slot], here, a2a_send.at[c, slot], a2a_recv.at[c, slot], peer)

    def scatter_part(c, slots):
        for slot in slots:
            base = others[slot][0] * share
            pick(send.at[c, slot], sending, base, mat, 6, 2 * c, share)
            a2a(c, slot).start()
        if 2 in slots:
            mine = recv[c].at[pl.ds(pl.multiple_of(p * (2 * share), 8), 2 * share)]
            pick(mine, sending, p * share, mat, 6, 2 * c, share)

    def collect_chunk(c):
        for slot in range(3):
            a2a(c, slot).wait_recv()
        pick(work.at[c], taking, 0, recv[c], 2, 0, local_rows)

    def top_of(c, owner):
        return tops.at[c, pl.ds(pl.multiple_of(owner * top, 8), top)]

    def gather_own(c):
        own = work.at[c, pl.ds(0, top)]
        copy = pltpu.make_async_copy(own, top_of(c, p), local_sem.at[c])
        copy.start()

        @pl.when(p < 3)
        def _():
            remote(own, top_of(c, p), ag_send.at[c, 0, 0], ag_recv.at[c, 0, 0], (p + 1, q)).start()

        @pl.when(p > 0)
        def _():
            remote(own, top_of(c, p), ag_send.at[c, 1, 0], ag_recv.at[c, 1, 0], (p - 1, q)).start()

    def gather_pass(c, dist):
        for way, step in ((0, 1), (1, -1)):
            owner = p - step * dist
            ahead = p + step

            @pl.when((owner >= 0) & (owner <= 3))
            def _():
                here = top_of(c, owner)
                remote(
                    here, here, ag_send.at[c, way, dist], ag_recv.at[c, way, dist - 1], (p, xq)
                ).wait_recv()

                @pl.when((ahead >= 0) & (ahead <= 3))
                def _():
                    remote(
                        here, here, ag_send.at[c, way, dist],
                        ag_recv.at[c, way, dist], (ahead, q),
                    ).start()

    def gather_sent(c):
        for way, step in ((0, 1), (1, -1)):
            ahead = p + step
            for dist in range(3):
                owner = p - step * dist

                @pl.when((owner >= 0) & (owner <= 3) & (ahead >= 0) & (ahead <= 3))
                def _():
                    here = top_of(c, owner)
                    remote(
                        here, here, ag_send.at[c, way, dist], ag_recv.at[c, way, dist], (p, xq)
                    ).wait_send()

    def gather_kept(c):
        pltpu.make_async_copy(work.at[c, pl.ds(0, top)], top_of(c, p), local_sem.at[c]).wait()

    straight = across * 2 + core
    cross = (1 - across) * 2 + core
    spots = [4 * top + 0, 4 * top + size, 4 * top + 2 * size, 0, size]

    def place(block, piece):
        return cols.at[block, pl.ds(spots[piece], size)]

    def first_source(piece):
        if piece < 3:
            return work.at[0, pl.ds(piece * size, size)]
        return tops.at[0, pl.ds((piece - 3) * size, size)]

    def to_x(src, piece):
        return remote(src, place(straight, piece), x_send.at[piece], x_recv.at[piece], (p, xq))

    def to_y(src, piece):
        return remote(src, place(straight, piece), y_send.at[piece], y_recv.at[piece], (p, yq))

    def to_s(src, kind, piece):
        block = (straight, cross)[kind]
        return remote(
            src, place(block, piece), s_send.at[kind, piece], s_recv.at[kind, piece], (p, sq)
        )

    def keep_own(piece):
        return pltpu.make_async_copy(
            first_source(piece), place(straight, piece), local_sem.at[3 + piece]
        )

    def column_start(piece):
        @pl.when(side == 0)
        def _():
            src = first_source(piece)
            to_y(src, piece).start()
            to_x(src, piece).start()
            to_s(src, 0, piece).start()
            keep_own(piece).start()

    def column_pass(piece):
        @pl.when(side == 1)
        def _():
            here = place(straight, piece)
            to_y(here, piece).wait_recv()
            to_x(here, piece).start()
            to_s(here, 0, piece).start()

        here = place(cross, piece)
        remote(here, here, x_send.at[piece], x_recv.at[piece], (p, xq)).wait_recv()
        to_s(here, 1, piece).start()

    def column_end(piece):
        for kind in range(2):
            block = (straight, cross)[kind]
            theirs = place(block + 1 - 2 * core, piece)
            remote(
                theirs, theirs, s_send.at[kind, piece], s_recv.at[kind, piece], (p, sq)
            ).wait_recv()
            to_s(theirs, kind, piece).wait_send()
        to_x(place(straight, piece), piece).wait_send()

        @pl.when(side == 0)
        def _():
            to_y(place(straight, piece), piece).wait_send()
            keep_own(piece).wait()

    scatter_part(0, (0, 1, 2))
    scatter_part(1, (0,))
    collect_chunk(0)
    for piece in range(3):
        column_start(piece)
    gather_own(0)
    scatter_part(1, (1, 2))
    column_pass(0)
    gather_pass(0, 1)
    scatter_part(2, (0,))
    column_pass(1)
    gather_pass(0, 2)
    scatter_part(2, (1, 2))
    collect_chunk(1)
    gather_own(1)
    column_pass(2)
    gather_pass(0, 3)
    gather_kept(0)
    column_start(3)
    column_start(4)
    gather_pass(1, 1)
    collect_chunk(2)
    gather_own(2)
    gather_pass(1, 2)
    column_pass(3)
    gather_pass(2, 1)
    gather_pass(1, 3)
    gather_pass(2, 2)
    column_pass(4)
    gather_pass(2, 3)
    gather_kept(1)
    gather_kept(2)
    for c in range(3):
        gather_sent(c)
    for piece in range(5):
        column_end(piece)
    for c in range(3):
        for slot in range(3):
            a2a(c, slot).wait_send()


def exchange(matrix, sending, taking, nrows, width):
    local_rows = nrows * width
    share = local_rows // 4
    dma = pltpu.SemaphoreType.DMA
    vmem = pl.BlockSpec(memory_space=pltpu.VMEM)
    smem = pl.BlockSpec(memory_space=pltpu.SMEM)
    hbm = pl.BlockSpec(memory_space=pl.ANY)
    f32 = jnp.float32
    return pl.pallas_call(
        functools.partial(exchange_kernel, nrows, width),
        out_shape=(
            jax.ShapeDtypeStruct((3, 2 * local_rows, 128), f32),
            jax.ShapeDtypeStruct((3, 8 * width, 128), f32),
            jax.ShapeDtypeStruct((4, 8 * width + 2 * local_rows, 128), f32),
        ),
        in_specs=[smem, smem, vmem],
        out_specs=(vmem, hbm, hbm),
        scratch_shapes=[
            pltpu.VMEM((3, 3, 2 * share, 128), f32),
            pltpu.VMEM((2 * local_rows, 128), f32),
            pltpu.VMEM((2 * local_rows, 128), f32),
            pltpu.VMEM((2 * local_rows, 128), f32),
            dma((3, 3)), dma((3, 3)), dma((3, 2, 4)), dma((3, 2, 4)),
            dma((5,)), dma((5,)), dma((5,)), dma((5,)), dma((2, 5)), dma((2, 5)), dma((8,)),
        ],
        compiler_params=pltpu.CompilerParams(
            collective_id=0, has_side_effects=True, vmem_limit_bytes=60 * 1024 * 1024
        ),
        name="exchange",
    )(sending, taking, matrix)


def halves(x):
    high = x.astype(jnp.bfloat16)
    return high, (x - high.astype(jnp.float32)).astype(jnp.bfloat16)


def left3(x):
    high, rest = halves(x)
    return jnp.concatenate([high, high, rest], axis=1)


def right3(x):
    high, rest = halves(x)
    return jnp.concatenate([high, rest, high], axis=0)


def factor_kernel(
    nrows, width, lower_fill, upper_fill, work_in, tops_in, cols_in, inv, out, l3, u3, c3,
    work, tops, cols, sems,
):
    col_copies = [
        pltpu.make_async_copy(cols_in.at[k], cols.at[k], sems.at[k]) for k in range(4)
    ]
    top_copies = [
        pltpu.make_async_copy(tops_in.at[c], tops.at[c], sems.at[4 + c]) for c in range(3)
    ]
    work_copies = [
        pltpu.make_async_copy(work_in.at[c], work.at[c], sems.at[7 + c]) for c in range(3)
    ]
    for copy in col_copies[:1] + top_copies + col_copies[1:] + work_copies:
        copy.start()
    p = lax.axis_index("prow")
    q = lax.axis_index("pcol")

    def dot(a, b):
        return jnp.dot(a, b, preferred_element_type=jnp.float32)

    def kept(fill, k, block):
        return (block > k) & (fill[k, block] == 1)

    def pairs(ref, lead, start, rows):
        left = ref[lead, pl.ds(start, rows, stride=2), :]
        right = ref[lead, pl.ds(start + 1, rows, stride=2), :]
        return jnp.concatenate([left, right], axis=1)

    corner = 4 * width
    for k in range(4):
        deep = 3 * k * width
        inverse = right3(inv[k])
        col_copies[k].wait()

        def finish(h, start, keep):
            low = jnp.where(keep, dot(left3(h), inverse), 0.0)
            l3[pl.ds(start, width), deep : deep + 3 * width] = left3(low)

        for r in range(4):
            h = pairs(cols, k, 2 * r * width, width)
            take = 3 * min(r, k) * width
            if take:
                h = h - dot(l3[r * width : (r + 1) * width, :take], c3[:take, :])
            if r < k:
                c3[3 * r * width : 3 * (r + 1) * width, :] = right3(
                    jnp.where(kept(upper_fill, r, k), h, 0.0)
                )
            finish(h, r * width, kept(lower_fill, k, r))

        def tile(i, carry):
            start = pl.multiple_of(corner + i * width, width)
            h = pairs(cols, k, 2 * start, width)
            if deep:
                h = h - dot(l3[pl.ds(start, width), :deep], c3[:deep, :])
            finish(h, start, kept(lower_fill, k, i * 4 + p))
            return carry

        lax.fori_loop(0, nrows, tile, 0)
        for c in range(3):
            span = slice(c * width, (c + 1) * width)
            if k == 0:
                top_copies[c].wait()
            u = pairs(tops, c, 2 * k * width, width)
            if deep:
                u = u - dot(l3[k * width : (k + 1) * width, :deep], u3[:deep, span])
            u3[deep : deep + 3 * width, span] = right3(
                jnp.where(kept(upper_fill, k, c * 8 + q), u, 0.0)
            )

    def update(i, carry):
        start = pl.multiple_of(corner + i * width, width)
        for c in range(3):
            span = slice(c * width, (c + 1) * width)
            value = pairs(work, c, 2 * width * i, width) - dot(
                l3[pl.ds(start, width), :], u3[:, span]
            )
            if c == 0:
                for k in range(4):
                    deep = 3 * k * width
                    high = l3[pl.ds(start, width), deep : deep + width].astype(jnp.float32)
                    rest = l3[pl.ds(start, width), deep + 2 * width : deep + 3 * width]
                    low = high + rest.astype(jnp.float32)
                    value = jnp.where((q == k) & (i * 4 + p > k), low, value)
            for half in range(2):
                out[pl.ds(i * (6 * width) + 2 * c + half, width, stride=6), :] = value[
                    :, half * 128 : (half + 1) * 128
                ]
        return carry

    for copy in work_copies:
        copy.wait()
    lax.fori_loop(0, nrows, update, 0)


def factor(lower_fill, upper_fill, work, tops, cols, inverses, nrows, width):
    vmem = pl.BlockSpec(memory_space=pltpu.VMEM)
    smem = pl.BlockSpec(memory_space=pltpu.SMEM)
    rows = (4 + nrows) * width
    bf16 = jnp.bfloat16
    return pl.pallas_call(
        functools.partial(factor_kernel, nrows, width),
        out_shape=jax.ShapeDtypeStruct((nrows * width * 6, 128), jnp.float32),
        in_specs=[smem] * 2 + [pl.BlockSpec(memory_space=pl.ANY)] * 3 + [vmem],
        out_specs=vmem,
        scratch_shapes=[
            pltpu.VMEM((rows, 12 * width), bf16),
            pltpu.VMEM((12 * width, 3 * width), bf16),
            pltpu.VMEM((12 * width, width), bf16),
            pltpu.VMEM(work.shape, jnp.float32),
            pltpu.VMEM(tops.shape, jnp.float32),
            pltpu.VMEM(cols.shape, jnp.float32),
            pltpu.SemaphoreType.DMA((10,)),
        ],
        compiler_params=pltpu.CompilerParams(vmem_limit_bytes=60 * 1024 * 1024),
        name="factor",
    )(lower_fill, upper_fill, work, tops, cols, inverses)


def kernel_body(matrix, row_order, inverses, lower_fill, upper_fill):
    nrows, width = matrix.shape[0], matrix.shape[2]
    p = lax.axis_index("prow")
    sending, taking = index_lists(row_order, nrows, width, 4, p)
    linear = matrix.reshape(nrows * width * 6, 128)
    work, tops, cols = exchange(linear, sending, taking, nrows, width)
    out = factor(lower_fill, upper_fill, work, tops, cols, inverses, nrows, width)
    return out.reshape(matrix.shape)


def solution(mesh):
    in_specs = (P(None, "prow", None, None, "pcol", None), P(), P(), P(), P())
    out_specs = P(None, "prow", None, None, "pcol", None)
    fits = mesh.shape["prow"] == 4 and mesh.shape["pcol"] == 8
    return jax.shard_map(
        kernel_body if fits else body,
        mesh=mesh, in_specs=in_specs, out_specs=out_specs, check_vma=False,
    )
```

profile of v0, /device:TPU:28, one launch (start us, length us, event | category | flops | bytes accessed | tf_op | source)
XLA Modules:
  0.0 212.9 jit_solution(1488092597205971817)
XLA Ops:
  0.0 0.8 reshape.45
  0.9 0.3 reduce-window.9
  1.2 0.1 slice.21
  1.3 0.1 reduce-window.12
  1.3 0.1 slice_reduce_fusion
  1.5 0.1 fusion.6
  1.6 5.6 %sort.7 = s32[7680]{0:T(1024)S(1)} sort(s32[7680]{0:T(1024)S(1)} %pad_add_fusion), dimensions={0}, to_apply=%region_2.3 | sort | flops 99840 | bytes 61440 | tf_op jit(solution)/shard_map/sort | solution.py:27
  7.2 0.6 fusion.20
  7.8 170.7 %exchange.1 = (f32[3,3072,128]{2,1,0:T(8,128)}, f32[3,2048,128]{2,1,0:T(8,128)}, f32[4,5120,128]{2,1,0:T(8,128)}) custom-call(s32[1536]{0:T(1024)} %get-tuple-element.12.sending, s32[1536]{0:T(1024)} %get-tuple-element.11.taking, f32[9216,128]{1,0:T(8,128)} %bitcast.5), custom_call_target="tpu_custom_call" | custom-call | tf_op jit(solution)/shard_map/exchange/pallas_call | solution.py:328
  178.5 34.4 %factor.1 = f32[9216,128]{1,0:T(8,128)} custom-call(s32[4,24]{1,0:T(4,128)} %lower_fill.1, s32[4,24]{1,0:T(4,128)} %upper_fill.1, f32[3,3072,128]{2,1,0:T(8,128)} %get-tuple-element.8.work_in, f32[3,2048,128]{2,1,0:T(8,128)} %get-tuple-element.9.tops_in, f32[4,5120,128]{2,1,0:T(8,128)} %get-tuple-element.10.cols_in, f32[4,256,256]{2,1,0:T(8,128)} %inv.1), custom_call_target="tpu_custom_call" | custom-call | tf_op jit(solution)/shard_map/factor/pallas_call | solution.py:467
  (9 shorter events, 0.1 us)
where the time goes:
time: 216 us; the launch traced here: 213 us
  Pallas kernels  205 us (95%)
  other arithmetic  6.13 us (3%)
    pallas_call x1, Pallas kernels, exchange(): pl.pallas_call(functools.partial(exchange_kernel, nrows, width), out_shap...  171 us
    pallas_call x1, Pallas kernels, factor(): pl.pallas_call(functools.partial(factor_kernel, nrows, width), out_shape=...  34.4 us
    sort x1, other arithmetic, index_lists(): both = lax.sort(both, is_stable=False)[:2 * local_rows] % local_rows  5.6 us

commit v1 on v0

v1 whole, which is shorter than its diff:
```python
import functools

import jax
import jax.numpy as jnp
from jax import lax
from jax.experimental import pallas as pl
from jax.experimental.pallas import tpu as pltpu
from jax.sharding import PartitionSpec as P


def mm(a, b):
    return jnp.dot(a, b, precision=lax.Precision.HIGH, preferred_element_type=jnp.float32)


def index_lists(row_order, rows, width, prows, here_row):
    local_rows = rows * width
    blocks = row_order.reshape(rows, prows, width)
    targets = lax.dynamic_index_in_dim(blocks, here_row, 1, keepdims=False).reshape(-1)
    local = jnp.arange(local_rows, dtype=jnp.int32)
    sending = (targets // width % prows) * local_rows + local
    by_source = jnp.transpose(blocks, (1, 0, 2)).reshape(-1)
    dest_local = by_source // width // prows * width + by_source % width
    mine = by_source // width % prows == here_row
    position = jnp.cumsum(mine.astype(jnp.int32)) - 1
    key = jnp.where(mine, dest_local * local_rows + position, local_rows * local_rows)
    both = jnp.concatenate([sending, prows * local_rows + key])
    both = lax.sort(both, is_stable=False)[: 2 * local_rows] % local_rows
    return both[:local_rows], both[local_rows:]


def keep_of(fill_row, panel, blocks):
    return (blocks > panel) & (fill_row[blocks] == 1)


def body(matrix, row_order, inverses, lower_fill, upper_fill):
    nrows = matrix.shape[0]
    width = matrix.shape[2]
    ncols = matrix.shape[3]
    prows = lax.axis_size("prow")
    pcols = lax.axis_size("pcol")
    p = lax.axis_index("prow")
    q = lax.axis_index("pcol")
    panels = inverses.shape[0]
    local_rows = nrows * width
    cols = ncols * width
    sending, taking = index_lists(row_order, nrows, width, prows, p)
    work = matrix.reshape(local_rows, cols)
    outgoing = work[sending].reshape(prows, local_rows // prows, cols)
    incoming = lax.all_to_all(outgoing, "prow", split_axis=0, concat_axis=0, tiled=True)
    work = incoming.reshape(local_rows, cols)[taking]
    tops = lax.all_gather(work[:width], "prow", axis=0, tiled=False)[:panels]
    tops = tops.reshape(panels * width, cols)
    column = jnp.concatenate([tops[:, :width], work[:, :width]], axis=0)
    ratio = pcols // panels
    pieces = column.reshape(ratio, -1, width)
    piece = jnp.where(q < panels, pieces[0], 0.0)
    for j in range(1, ratio):
        pairs = [(k, k + panels * j) for k in range(panels)]
        piece = piece + lax.ppermute(pieces[j], "pcol", pairs)
    every = lax.all_gather(piece, "pcol", axis=0, tiled=False)
    every = every.reshape(ratio, panels, piece.shape[0], width)
    columns = [every[:, k].reshape(column.shape) for k in range(panels)]
    row_blocks = jnp.concatenate(
        [jnp.arange(panels, dtype=jnp.int32), jnp.arange(nrows, dtype=jnp.int32) * prows + p]
    )
    col_blocks = jnp.arange(ncols, dtype=jnp.int32) * pcols + q
    corner = panels * width
    lowers, uppers = [], []
    mine = work[:, :width]
    for k in range(panels):
        here = columns[k]
        for m in range(k):
            keep = (upper_fill[m, k] == 1).astype(jnp.float32)
            part = here[m * width : (m + 1) * width] * keep
            here = here - mm(lowers[m], part)
        columns[k] = here
        row_keep = jnp.repeat(keep_of(lower_fill[k], k, row_blocks), width)[:, None]
        lower = jnp.where(row_keep, mm(here, inverses[k]), 0.0)
        lowers.append(lower)
        row = tops[k * width : (k + 1) * width]
        for m in range(k):
            row = row - mm(lower_rows(lowers[m], k, width), uppers[m])
        col_keep = jnp.repeat(keep_of(upper_fill[k], k, col_blocks), width)[None, :]
        uppers.append(jnp.where(col_keep, row, 0.0))
    left = jnp.concatenate([x[corner:] for x in lowers], axis=1)
    out = work - mm(left, jnp.concatenate(uppers, axis=0))
    row_ids = jnp.repeat(row_blocks[panels:], width)[:, None]
    first = out[:, :width]
    for k in range(panels):
        first = jnp.where((q == k) & (row_ids > k), lowers[k][corner:], first)
    out = out.at[:, :width].set(first)
    return out.reshape(nrows, 1, width, ncols, 1, width)


def lower_rows(lower, k, width):
    return lower[k * width : (k + 1) * width]


MESH = pl.DeviceIdType.MESH


def tables(row_order, rows, width, here_row):
    local_rows = rows * width
    share = local_rows // 4
    blocks = row_order.reshape(rows, 4, width)
    targets = lax.dynamic_index_in_dim(blocks, here_row, 1, keepdims=False).reshape(-1)
    local = jnp.arange(local_rows, dtype=jnp.int32)
    late = (targets >= 4 * width).astype(jnp.int32)
    sending = (targets // width % 4 * 2 + late) * local_rows + local
    by_source = jnp.transpose(blocks, (1, 0, 2)).reshape(4, local_rows)
    mine = by_source // width % 4 == here_row
    first = mine & (by_source < 4 * width)
    firsts = jnp.cumsum(first.astype(jnp.int32), axis=1)
    lates = jnp.cumsum((mine & ~first).astype(jnp.int32), axis=1)
    rank = jnp.where(first, firsts, firsts[:, -1:] + lates) - 1
    position = jnp.arange(4, dtype=jnp.int32)[:, None] * share + rank
    dest_local = by_source // width // 4 * width + by_source % width
    key = jnp.where(mine, dest_local * local_rows + position, local_rows * local_rows)
    both = jnp.concatenate([sending, 8 * local_rows + key.reshape(-1)])
    both = lax.sort(both, is_stable=False)[: 2 * local_rows] % local_rows
    taking = both[local_rows:]
    head = taking[:width]
    return both[:local_rows], taking, head // share * width + head % share


def halves(x):
    high = x.astype(jnp.bfloat16)
    return high, (x - high.astype(jnp.float32)).astype(jnp.bfloat16)


def dot3(a, b):
    def dot(x, y):
        return jnp.dot(x, y, preferred_element_type=jnp.float32)

    return dot(a[0], b[0]) + dot(a[0], b[1]) + dot(a[1], b[0])


def fused_kernel(
    nrows, width, sending, taking, heads, lower_fill, upper_fill, mat_in, inv, out,
    mat, send, early0, early1, early2, all0, all1, all2, work, tops, cols,
    lh, ll, uh, ul, ch, cl, ih, il,
    a2a_send, a2a_recv, g_send, g_recv, x_send, x_recv, y_send, y_recv, s_send, s_recv,
    keep_sem, join_sem, mat_sem,
):
    p = lax.axis_index("prow")
    q = lax.axis_index("pcol")
    side, across, core = q // 4, q // 2 % 2, q % 2
    xq = side * 4 + (1 - across) * 2 + core
    yq = (1 - side) * 4 + across * 2 + core
    sq = side * 4 + across * 2 + (1 - core)
    local_rows = nrows * width
    share = local_rows // 4
    top = 2 * width
    size = 4 * width
    span6 = 6 * width
    late = 2 * (share - width)
    partner = p + 1 - 2 * (p % 2)
    others = [((p + 2) % 4, q), (3 - p, q), (partner, q)]
    early = (early0, early1, early2)
    full = (all0, all1, all2)

    load = pltpu.make_async_copy(mat_in, mat, mat_sem.at[6])
    load.start()
    barrier = pltpu.get_barrier_semaphore()
    for peer in others + [(p, xq), (p, yq), (p, sq)]:
        pl.semaphore_signal(barrier, inc=1, device_id=peer, device_id_type=MESH)
    pl.semaphore_wait(barrier, 6)
    load.wait()

    def remote(src, dst, send_sem, recv_sem, peer):
        return pltpu.make_async_remote_copy(
            src_ref=src, dst_ref=dst, send_sem=send_sem, recv_sem=recv_sem,
            device_id=peer, device_id_type=MESH,
        )

    def pick(dst, index, index_base, source, pitch, offset, count):
        unroll = 8

        def group(g, carry):
            for u in range(unroll):
                row = index[index_base + g * unroll + u]
                dst[pl.ds(g * (2 * unroll) + 2 * u, 2), :] = source[
                    pl.ds(row * pitch + offset, 2), :
                ]
            return carry

        lax.fori_loop(0, count // unroll, group, 0)

    def a2a(c, slot, part):
        if part == 0:
            src = send.at[c, slot, pl.ds(0, top)]
            dst = early[c].at[pl.ds(pl.multiple_of(p * top, 8), top)]
        else:
            src = send.at[c, slot, pl.ds(top, late)]
            dst = full[c].at[pl.ds(pl.multiple_of(p * (2 * share) + top, 8), late)]
        return remote(
            src, dst, a2a_send.at[c, slot, part], a2a_recv.at[c, slot, part], others[slot]
        )

    def pick_send(c, slot, part):
        base = others[slot][0] * share
        if part == 0:
            pick(send.at[c, slot, pl.ds(0, top)], sending, base, mat, 6, 2 * c, width)
        else:
            pick(
                send.at[c, slot, pl.ds(top, late)], sending, base + width, mat, 6, 2 * c,
                share - width,
            )

    def pick_mine(c):
        here = early[c].at[pl.ds(pl.multiple_of(p * top, 8), top)]
        pick(here, sending, p * share, mat, 6, 2 * c, width)
        here = full[c].at[pl.ds(pl.multiple_of(p * (2 * share) + top, 8), late)]
        pick(here, sending, p * share + width, mat, 6, 2 * c, share - width)

    def start(c, slots, part):
        for slot in slots:
            a2a(c, slot, part).start()

    def join(c, s):
        return pltpu.make_async_copy(
            early[c].at[pl.ds(s * top, top)], full[c].at[pl.ds(s * 2 * share, top)],
            join_sem.at[c, s],
        )

    def top_of(c, owner):
        return tops.at[c, pl.ds(pl.multiple_of(owner * top, 8), top)]

    def early_in(c):
        for slot in range(3):
            a2a(c, slot, 0).wait_recv()
        for s in range(4):
            join(c, s).start()
        pick(top_of(c, p), heads, 0, early[c], 2, 0, width)

    def late_in(c):
        for slot in range(3):
            a2a(c, slot, 1).wait_recv()
        for s in range(4):
            join(c, s).wait()

    cross = (2 - p // 2, q)
    inner = (p == 1) | (p == 2)
    outer = (p == 0) | (p == 3)
    far = 2 - 2 * (p // 2)

    def gather_copy(c, owner, sem, peer):
        here = top_of(c, owner)
        return remote(here, here, g_send.at[c, sem], g_recv.at[c, owner], peer)

    def gather_start(c):
        gather_copy(c, p, 1, cross).start()
        gather_copy(c, p, 0, (partner, q)).start()

    def gather_relay(c):
        @pl.when(inner)
        def _():
            for j in range(2):
                gather_copy(c, far + j, 2 + j, (partner, q)).wait_recv()
                gather_copy(c, far + j, 2 + j, (partner, q)).start()

    def gather_end(c):
        gather_copy(c, partner, 0, (partner, q)).wait_recv()

        @pl.when(outer)
        def _():
            for j in range(2):
                gather_copy(c, far + j, 2 + j, (partner, q)).wait_recv()

    def gather_sent(c):
        gather_copy(c, p, 1, cross).wait_send()
        gather_copy(c, p, 0, (partner, q)).wait_send()

        @pl.when(inner)
        def _():
            for j in range(2):
                gather_copy(c, far + j, 2 + j, (partner, q)).wait_send()

    straight = across * 2 + core
    crossed = (1 - across) * 2 + core
    spots = [4 * top + 0, 4 * top + size, 4 * top + 2 * size, 0, size]

    def place(block, piece):
        return cols.at[block, pl.ds(spots[piece], size)]

    def first_source(piece):
        if piece < 3:
            return work.at[pl.ds(piece * size, size)]
        return tops.at[0, pl.ds((piece - 3) * size, size)]

    def to_x(src, piece):
        return remote(src, place(straight, piece), x_send.at[piece], x_recv.at[piece], (p, xq))

    def to_y(src, piece):
        return remote(src, place(straight, piece), y_send.at[piece], y_recv.at[piece], (p, yq))

    def to_s(src, kind, piece):
        block = (straight, crossed)[kind]
        return remote(
            src, place(block, piece), s_send.at[kind, piece], s_recv.at[kind, piece], (p, sq)
        )

    def keep_own(piece):
        return pltpu.make_async_copy(
            first_source(piece), place(straight, piece), keep_sem.at[piece]
        )

    def column_start(piece):
        @pl.when(side == 0)
        def _():
            src = first_source(piece)
            to_y(src, piece).start()
            to_x(src, piece).start()
            to_s(src, 0, piece).start()
            keep_own(piece).start()

    def column_pass(piece):
        @pl.when(side == 1)
        def _():
            here = place(straight, piece)
            to_y(here, piece).wait_recv()
            to_x(here, piece).start()
            to_s(here, 0, piece).start()

    def column_across(piece):
        here = place(crossed, piece)
        remote(here, here, x_send.at[piece], x_recv.at[piece], (p, xq)).wait_recv()
        to_s(here, 1, piece).start()

    def column_ready(piece):
        for kind in range(2):
            block = (straight, crossed)[kind]
            theirs = place(block + 1 - 2 * core, piece)
            remote(
                theirs, theirs, s_send.at[kind, piece], s_recv.at[kind, piece], (p, sq)
            ).wait_recv()

        @pl.when(side == 0)
        def _():
            keep_own(piece).wait()

    def column_sent(piece):
        for kind in range(2):
            block = (straight, crossed)[kind]
            to_s(place(block, piece), kind, piece).wait_send()
        to_x(place(straight, piece), piece).wait_send()

        @pl.when(side == 0)
        def _():
            to_y(place(straight, piece), piece).wait_send()

    def kept(fill, k, block):
        return jnp.where((block > k) & (fill[k, block] == 1), 1.0, 0.0)

    def column_tile(k, start):
        left = cols[k, pl.ds(2 * start, width, stride=2), :]
        right = cols[k, pl.ds(2 * start + 1, width, stride=2), :]
        return jnp.concatenate([left, right], axis=1)

    def lower_of(start, deep):
        rows = pl.ds(start, width)
        return lh[rows, :deep], ll[rows, :deep]

    def put_lower(start, k, h, keep):
        rows, here = pl.ds(start, width), slice(k * width, (k + 1) * width)
        inverse = ih[here, :], il[here, :]
        lh[rows, here], ll[rows, here] = halves(dot3(halves(h), inverse) * keep)

    def corner():
        for r in range(4):
            for k in range(4):
                if k == r:
                    continue
                h = column_tile(k, r * width)
                deep = min(r, k) * width
                if deep:
                    h = h - dot3(lower_of(r * width, deep), (ch[k, :deep, :], cl[k, :deep, :]))
                if k < r:
                    put_lower(r * width, k, h, kept(lower_fill, k, r))
                else:
                    here = slice(r * width, (r + 1) * width)
                    ch[k, here, :], cl[k, here, :] = halves(h * kept(upper_fill, r, k))

    def panels(piece):
        for k in range(4):
            for i in (2 * piece, 2 * piece + 1):
                begin = (4 + i) * width
                h = column_tile(k, begin)
                deep = k * width
                if deep:
                    h = h - dot3(lower_of(begin, deep), (ch[k, :deep, :], cl[k, :deep, :]))
                put_lower(begin, k, h, kept(lower_fill, k, i * 4 + p))

    def upper(c):
        span = slice(c * width, (c + 1) * width)
        for r in range(4):
            left = tops[c, pl.ds(2 * r * width, width, stride=2), :]
            right = tops[c, pl.ds(2 * r * width + 1, width, stride=2), :]
            u = jnp.concatenate([left, right], axis=1)
            deep = r * width
            if deep:
                u = u - dot3(lower_of(r * width, deep), (uh[:deep, span], ul[:deep, span]))
            here = slice(r * width, (r + 1) * width)
            uh[here, span], ul[here, span] = halves(u * kept(upper_fill, r, c * 8 + q))

    def update(c):
        span = slice(c * width, (c + 1) * width)

        def tile(i, carry):
            begin = pl.multiple_of((4 + i) * width, width)
            value = dot3(lower_of(begin, 4 * width), (uh[:, span], ul[:, span]))
            if c == 0:
                at = pl.multiple_of(i * (2 * width), 8)
                old = jnp.concatenate(
                    [
                        work[pl.ds(at, width, stride=2), :],
                        work[pl.ds(at + 1, width, stride=2), :],
                    ],
                    axis=1,
                )
                value = old - value
                for k in range(4):
                    here = slice(k * width, (k + 1) * width)
                    rows = pl.ds(begin, width)
                    low = lh[rows, here].astype(jnp.float32) + ll[rows, here].astype(jnp.float32)
                    value = jnp.where((q == k) & (i * 4 + p > k), low, value)
            for half in range(2):
                part = value[:, half * 128 : (half + 1) * 128]
                rows = pl.ds(i * span6 + 2 * c + half, width, stride=6)
                if c == 1:
                    part = mat[rows, :] - part
                mat[rows, :] = part
            return carry

        lax.fori_loop(0, nrows, tile, 0)

    def take(c, subtract, first, count):
        def group(g, carry):
            for u in range(8):
                row = taking[first + g * 8 + u]
                value = full[c][pl.ds(row * 2, 2), :]
                here = pl.ds((first + g * 8) * 6 + u * 6 + 2 * c, 2)
                if subtract:
                    value = value - mat[here, :]
                mat[here, :] = value
            return carry

        lax.fori_loop(0, count // 8, group, 0)

    for slot in range(3):
        pick_send(0, slot, 0)
        start(0, (slot,), 0)
    for slot in range(3):
        pick_send(0, slot, 1)
        start(0, (slot,), 1)
    pick_mine(0)
    for c in (1, 2):
        for part in range(2):
            for slot in range(3):
                pick_send(c, slot, part)
        pick_mine(c)
    ih[...], il[...] = halves(inv[...])
    early_in(0)
    gather_start(0)
    start(1, (0, 1, 2), 0)
    late_in(0)
    pick(work, taking, 0, all0, 2, 0, local_rows)
    column_start(0)
    gather_relay(0)
    start(1, (0, 1, 2), 1)
    gather_end(0)
    column_start(3)
    column_start(4)
    column_start(1)
    column_start(2)
    column_pass(0)
    column_across(0)
    column_pass(3)
    column_across(3)
    early_in(1)
    gather_start(1)
    start(2, (0, 1, 2), 0)
    start(2, (0,), 1)
    column_pass(4)
    column_across(4)
    late_in(1)
    take(1, False, 0, local_rows)
    gather_relay(1)
    column_pass(1)
    column_ready(3)
    column_ready(4)
    corner()
    column_across(1)
    column_pass(2)
    column_ready(0)
    panels(0)
    column_across(2)
    gather_end(1)
    column_ready(1)
    panels(1)
    early_in(2)
    gather_start(2)
    start(2, (1, 2), 1)
    upper(0)
    upper(1)
    column_ready(2)
    panels(2)
    gather_relay(2)
    update(0)
    update(1)
    gather_end(2)
    upper(2)
    update(2)
    late_in(2)

    def leave(i):
        rows = pl.ds(i * span6, span6)
        return pltpu.make_async_copy(mat.at[rows], out.at[rows], mat_sem.at[i])

    for i in range(nrows):
        take(2, True, i * width, width)
        leave(i).start()
    for c in range(3):
        gather_sent(c)
        for slot in range(3):
            for part in range(2):
                a2a(c, slot, part).wait_send()
    for piece in range(5):
        column_sent(piece)
    for i in range(nrows):
        leave(i).wait()


def fused(matrix, sending, taking, heads, lower_fill, upper_fill, inverses, nrows, width):
    local_rows = nrows * width
    share = local_rows // 4
    dma = pltpu.SemaphoreType.DMA
    vmem = pl.BlockSpec(memory_space=pltpu.VMEM)
    smem = pl.BlockSpec(memory_space=pltpu.SMEM)
    hbm = pl.BlockSpec(memory_space=pl.ANY)
    f32, bf16 = jnp.float32, jnp.bfloat16
    rows = (4 + nrows) * width
    return pl.pallas_call(
        functools.partial(fused_kernel, nrows, width),
        out_shape=jax.ShapeDtypeStruct((6 * local_rows, 128), f32),
        in_specs=[smem] * 5 + [hbm, vmem],
        out_specs=hbm,
        scratch_shapes=[
            pltpu.VMEM((6 * local_rows, 128), f32),
            pltpu.VMEM((3, 3, 2 * share, 128), f32),
            *[pltpu.VMEM((8 * width, 128), f32)] * 3,
            *[pltpu.VMEM((2 * local_rows, 128), f32)] * 3,
            pltpu.VMEM((2 * local_rows, 128), f32),
            pltpu.VMEM((3, 8 * width, 128), f32),
            pltpu.VMEM((4, 8 * width + 2 * local_rows, 128), f32),
            *[pltpu.VMEM((rows, 4 * width), bf16)] * 2,
            *[pltpu.VMEM((4 * width, 3 * width), bf16)] * 2,
            *[pltpu.VMEM((4, 3 * width, width), bf16)] * 2,
            *[pltpu.VMEM((4 * width, width), bf16)] * 2,
            dma((3, 3, 2)), dma((3, 3, 2)), dma((3, 4)), dma((3, 4)),
            dma((5,)), dma((5,)), dma((5,)), dma((5,)), dma((2, 5)), dma((2, 5)),
            dma((5,)), dma((3, 4)), dma((7,)),
        ],
        compiler_params=pltpu.CompilerParams(
            collective_id=0, has_side_effects=True, vmem_limit_bytes=63 * 1024 * 1024
        ),
        name="fused",
    )(sending, taking, heads, lower_fill, upper_fill, matrix, inverses.reshape(-1, width))


def kernel_body(matrix, row_order, inverses, lower_fill, upper_fill):
    nrows, width = matrix.shape[0], matrix.shape[2]
    p = lax.axis_index("prow")
    sending, taking, heads = tables(row_order, nrows, width, p)
    linear = matrix.reshape(nrows * width * 6, 128)
    out = fused(linear, sending, taking, heads, lower_fill, upper_fill, inverses, nrows, width)
    return out.reshape(matrix.shape)


def solution(mesh):
    in_specs = (P(None, "prow", None, None, "pcol", None), P(), P(), P(), P())
    out_specs = P(None, "prow", None, None, "pcol", None)
    fits = mesh.shape["prow"] == 4 and mesh.shape["pcol"] == 8
    return jax.shard_map(
        kernel_body if fits else body,
        mesh=mesh, in_specs=in_specs, out_specs=out_specs, check_vma=False,
    )
```

time: 216 us -> 200 us (0.926); the launches traced: 213 us -> 200 us
  Pallas kernels: 205 us -> 181 us
  local copies, waits for them, and re-layouts: 1.59 us -> 10 us
  other arithmetic: 6.13 us -> 9.26 us
    pallas_call x2 -> x1, Pallas kernels: 205 us -> 181 us  [fused(): pl.pallas_call(functools.partial(fused_kernel, nrows, width), out_shape=j...]
    unnamed x0 -> x2, local copies, waits for them, and re-layouts: none -> 7.78 us
    another operation x2 -> x6, other arithmetic: 0.36 us -> 2.83 us
where the time goes in v1:
time: 200 us
  Pallas kernels  181 us (90%)
  local copies, waits for them, and re-layouts  10 us (5%)
  other arithmetic  9.26 us (5%)
    pallas_call x1, Pallas kernels, fused(): pl.pallas_call(functools.partial(fused_kernel, nrows, width), out_shape=j...  181 us
    unnamed x2, local copies, waits for them, and re-layouts  7.78 us
    sort x1, other arithmetic, tables(): both = lax.sort(both, is_stable=False)[:2 * local_rows] % local_rows  5.6 us

profile of v1, /device:TPU:28, one launch (start us, length us, event | category | flops | bytes accessed | tf_op | source)
XLA Modules:
  0.0 200.1 jit_solution(13323362067283820263)
XLA Ops:
  0.0 0.1 add.102
  0.1 0.8 reshape.79
  1.0 1.2 reduce-window.16
  2.2 0.2 slice_reduce_fusion
  2.4 0.2 reduce-window.19
  2.6 0.1 broadcast_add_fusion
  2.7 1.2 reduce-window.14
  3.8 0.2 slice_reduce_fusion.1
  4.1 0.2 reduce-window.15
  4.2 0.1 fusion.23
  4.4 0.1 broadcast_add_fusion.1
  4.4 0.2 slice_reduce_fusion.2
  4.6 0.1 add.106
  4.7 0.1 fusion.10
  4.8 5.6 %sort.7 = s32[7680]{0:T(1024)S(1)} sort(s32[7680]{0:T(1024)S(1)} %pad_add_fusion), dimensions={0}, to_apply=%region_4.5 | sort | flops 99840 | bytes 61440 | tf_op jit(solution)/shard_map/sort | solution.py:120
  10.4 0.6 fusion.21.heads
  11.0 0.6 fusion.22
  11.6 180.7 %fused.1 = f32[9216,128]{1,0:T(8,128)} custom-call(s32[1536]{0:T(1024)} %get-tuple-element.8.sending, s32[1536]{0:T(1024)} %get-tuple-element.7.taking, s32[256]{0:T(256)} %fusion.21.heads, s32[4,24]{1,0:T(4,128)} %lower_fill.1, s32[4,24]{1,0:T(4,128)} %upper_fill.1, f32[9216,128]{1,0:T(8,128)} %bitcast.12, f32[1024,256]{1,0:T(8,128)} %bitcast.13), custom_call_target="tpu_custom_call" | custom-call | tf_op jit(solution)/shard_map/fused/pallas_call | solution.py:543
  192.3 7.8 %copy.18 = f32[6,1,256,3,1,256]{5,4,3,2,1,0:T(1,128)} copy(f32[6,1,256,3,1,256]{5,4,3,2,1,0:T(1,128)} %bitcast.11) | data formatting | bytes 9437184
  (16 shorter events, 0.2 us)

commit v2 on v1

--- a/solution.py
+++ b/solution.py
@@ -99,28 +99,92 @@
 MESH = pl.DeviceIdType.MESH
 
 
-def tables(row_order, rows, width, here_row):
-    local_rows = rows * width
-    share = local_rows // 4
-    blocks = row_order.reshape(rows, 4, width)
-    targets = lax.dynamic_index_in_dim(blocks, here_row, 1, keepdims=False).reshape(-1)
-    local = jnp.arange(local_rows, dtype=jnp.int32)
-    late = (targets >= 4 * width).astype(jnp.int32)
-    sending = (targets // width % 4 * 2 + late) * local_rows + local
-    by_source = jnp.transpose(blocks, (1, 0, 2)).reshape(4, local_rows)
-    mine = by_source // width % 4 == here_row
-    first = mine & (by_source < 4 * width)
-    firsts = jnp.cumsum(first.astype(jnp.int32), axis=1)
-    lates = jnp.cumsum((mine & ~first).astype(jnp.int32), axis=1)
-    rank = jnp.where(first, firsts, firsts[:, -1:] + lates) - 1
-    position = jnp.arange(4, dtype=jnp.int32)[:, None] * share + rank
-    dest_local = by_source // width // 4 * width + by_source % width
-    key = jnp.where(mine, dest_local * local_rows + position, local_rows * local_rows)
-    both = jnp.concatenate([sending, 8 * local_rows + key.reshape(-1)])
-    both = lax.sort(both, is_stable=False)[: 2 * local_rows] % local_rows
-    taking = both[local_rows:]
-    head = taking[:width]
-    return both[:local_rows], taking, head // share * width + head % share
+def one_hot_sum(rows_of, lanes_of, values):
+    groups = rows_of.shape[0]
+    up = lax.broadcasted_iota(jnp.int32, (16, 128), 0)
+    across = lax.broadcasted_iota(jnp.int32, (128, 128), 0)
+    lefts, rights = [], []
+    for g in range(groups):
+        here = slice(g, g + 1)
+        hit = up == rows_of[here]
+        value = values[here]
+        parts = [jnp.where(hit, value % 128, 0), jnp.where(hit, value // 128, 0)]
+        lefts.append(jnp.concatenate(parts, axis=0).astype(jnp.float32).astype(jnp.bfloat16))
+        rights.append((across == lanes_of[here]).astype(jnp.float32).astype(jnp.bfloat16))
+    total = lax.dot_general(
+        jnp.concatenate(lefts, axis=1), jnp.concatenate(rights, axis=1),
+        (((1,), (1,)), ((), ())), preferred_element_type=jnp.float32,
+    ).astype(jnp.int32)
+    return total[:16] + 128 * total[16:]
+
+
+def tables_kernel(nrows, width, order, out):
+    p = lax.axis_index("prow")
+    per = width // 128
+    lines = nrows * per
+    share = nrows * width // 4
+    bf16 = jnp.bfloat16
+
+    def dot(a, b):
+        return jnp.dot(a, b, preferred_element_type=jnp.float32)
+
+    by_source = [
+        jnp.concatenate(
+            [order[(r * 4 + s) * per : (r * 4 + s + 1) * per, :] for r in range(nrows)], axis=0
+        )
+        for s in range(4)
+    ]
+    targets = by_source[0] * (p == 0).astype(jnp.int32)
+    for s in range(1, 4):
+        targets = targets + by_source[s] * (p == s).astype(jnp.int32)
+    arriving = jnp.concatenate(by_source, axis=0)
+    leaving = jnp.concatenate([targets] * 4, axis=0)
+    group = lax.broadcasted_iota(jnp.int32, (4 * lines, 128), 0) // lines
+    mine = arriving // width % 4 == p
+    theirs = leaving // width % 4 == group
+    ranks = []
+    up = lax.broadcasted_iota(jnp.int32, (4 * lines, 4 * lines), 0)
+    along = lax.broadcasted_iota(jnp.int32, (4 * lines, 4 * lines), 1)
+    same = up // lines == along // lines
+    before = (same & (along < up)).astype(jnp.float32).astype(bf16)
+    same = same.astype(jnp.float32).astype(bf16)
+    upto = lax.broadcasted_iota(jnp.int32, (128, 128), 0)
+    upto = upto <= lax.broadcasted_iota(jnp.int32, (128, 128), 1)
+    upto = upto.astype(jnp.float32).astype(bf16)
+    ones = jnp.ones((128, 128), bf16)
+    for mask, where in ((mine, arriving), (theirs, leaving)):
+        low = where < 4 * width
+        first = (mask & low).astype(jnp.float32).astype(bf16)
+        late = (mask & (where >= 4 * width)).astype(jnp.float32).astype(bf16)
+        firsts = dot(first, upto) + dot(dot(before, first).astype(bf16), ones)
+        lates = dot(late, upto) + dot(dot(before, late).astype(bf16), ones)
+        count = dot(dot(same, first).astype(bf16), ones)
+        rank = jnp.where(low, firsts, count + lates).astype(jnp.int32) - 1
+        ranks.append(group * share + rank)
+    dest = arriving // (4 * width) * width + arriving % width
+    row = jnp.where(mine, dest // 128, 15)
+    taking = one_hot_sum(row, dest % 128, ranks[0])
+    spot = jnp.where(theirs, ranks[1], 0)
+    spot = sum(spot[d * lines : (d + 1) * lines] for d in range(4))
+    local = lax.broadcasted_iota(jnp.int32, (lines, 128), 0) * 128
+    local = local + lax.broadcasted_iota(jnp.int32, (lines, 128), 1)
+    sending = one_hot_sum(spot // 128, spot % 128, local)
+    out[:16, :] = sending
+    out[16:32, :] = taking
+    source = sum((taking[:8] >= s * share).astype(jnp.int32) for s in (1, 2, 3))
+    out[32:40, :] = taking[:8] - source * (share - width)
+
+
+def tables(row_order, nrows, width):
+    vmem = pl.BlockSpec(memory_space=pltpu.VMEM)
+    return pl.pallas_call(
+        functools.partial(tables_kernel, nrows, width),
+        out_shape=jax.ShapeDtypeStruct((40, 128), jnp.int32),
+        in_specs=[vmem], out_specs=vmem, name="tables",
+    )(row_order.reshape(-1, 128)).reshape(-1)
+
+
+SENDING, TAKING, HEADS = 0, 2048, 4096
 
 
 def halves(x):
@@ -136,8 +200,8 @@
 
 
 def fused_kernel(
-    nrows, width, sending, taking, heads, lower_fill, upper_fill, mat_in, inv, out,
-    mat, send, early0, early1, early2, all0, all1, all2, work, tops, cols,
+    nrows, width, table, lower_fill, upper_fill, mat_in, inv, out, all2,
+    mat, send, early0, early1, early2, all0, all1, mine2, work, tops, cols,
     lh, ll, uh, ul, ch, cl, ih, il,
     a2a_send, a2a_recv, g_send, g_recv, x_send, x_recv, y_send, y_recv, s_send, s_recv,
     keep_sem, join_sem, mat_sem,
@@ -151,7 +215,6 @@
     local_rows = nrows * width
     share = local_rows // 4
     top = 2 * width
-    size = 4 * width
     span6 = 6 * width
     late = 2 * (share - width)
     partner = p + 1 - 2 * (p % 2)
@@ -173,12 +236,12 @@
             device_id=peer, device_id_type=MESH,
         )
 
-    def pick(dst, index, index_base, source, pitch, offset, count):
+    def pick(dst, index_base, source, pitch, offset, count):
         unroll = 8
 
         def group(g, carry):
             for u in range(unroll):
-                row = index[index_base + g * unroll + u]
+                row = table[index_base + g * unroll + u]
                 dst[pl.ds(g * (2 * unroll) + 2 * u, 2), :] = source[
                     pl.ds(row * pitch + offset, 2), :
                 ]
@@ -200,18 +263,27 @@
     def pick_send(c, slot, part):
         base = others[slot][0] * share
         if part == 0:
-            pick(send.at[c, slot, pl.ds(0, top)], sending, base, mat, 6, 2 * c, width)
+            pick(send.at[c, slot, pl.ds(0, top)], SENDING + base, mat, 6, 2 * c, width)
         else:
             pick(
-                send.at[c, slot, pl.ds(top, late)], sending, base + width, mat, 6, 2 * c,
+                send.at[c, slot, pl.ds(top, late)], SENDING + base + width, mat, 6, 2 * c,
                 share - width,
             )
 
+    def mine_copy():
+        here = pl.ds(pl.multiple_of(p * (2 * share) + top, 8), late)
+        return pltpu.make_async_copy(mine2, all2.at[here], mat_sem.at[7])
+
     def pick_mine(c):
+        base = SENDING + p * share
         here = early[c].at[pl.ds(pl.multiple_of(p * top, 8), top)]
-        pick(here, sending, p * share, mat, 6, 2 * c, width)
-        here = full[c].at[pl.ds(pl.multiple_of(p * (2 * share) + top, 8), late)]
-        pick(here, sending, p * share + width, mat, 6, 2 * c, share - width)
+        pick(here, base, mat, 6, 2 * c, width)
+        here = mine2
+        if c < 2:
+            here = full[c].at[pl.ds(pl.multiple_of(p * (2 * share) + top, 8), late)]
+        pick(here, base + width, mat, 6, 2 * c, share - width)
+        if c == 2:
+            mine_copy().start()
 
     def start(c, slots, part):
         for slot in slots:
@@ -231,7 +303,7 @@
             a2a(c, slot, 0).wait_recv()
         for s in range(4):
             join(c, s).start()
-        pick(top_of(c, p), heads, 0, early[c], 2, 0, width)
+        pick(top_of(c, p), HEADS, early[c], 2, 0, width)
 
     def late_in(c):
         for slot in range(3):
@@ -278,15 +350,19 @@
 
     straight = across * 2 + core
     crossed = (1 - across) * 2 + core
-    spots = [4 * top + 0, 4 * top + size, 4 * top + 2 * size, 0, size]
+    runs = [(i, min(2, nrows - i)) for i in range(1, nrows, 2)] + [(0, 2), (2, 2)]
+    owned = len(runs) - 2
 
     def place(block, piece):
-        return cols.at[block, pl.ds(spots[piece], size)]
+        first, count = runs[piece]
+        spot = first + 3 if piece < owned else first
+        return cols.at[block, pl.ds(spot * top, count * top)]
 
     def first_source(piece):
-        if piece < 3:
-            return work.at[pl.ds(piece * size, size)]
-        return tops.at[0, pl.ds((piece - 3) * size, size)]
+        first, count = runs[piece]
+        if piece < owned:
+            return work.at[pl.ds(first * top, count * top)]
+        return tops.at[0, pl.ds(first * top, count * top)]
 
     def to_x(src, piece):
         return remote(src, place(straight, piece), x_send.at[piece], x_recv.at[piece], (p, xq))
@@ -369,6 +445,10 @@
     def corner():
         for r in range(4):
             for k in range(4):
+                if k >= r:
+                    rows, there = pl.ds(r * width, width), slice(k * width, (k + 1) * width)
+                    lh[rows, there] = jnp.zeros((width, width), jnp.bfloat16)
+                    ll[rows, there] = jnp.zeros((width, width), jnp.bfloat16)
                 if k == r:
                     continue
                 h = column_tile(k, r * width)
@@ -383,8 +463,8 @@
 
     def panels(piece):
         for k in range(4):
-            for i in (2 * piece, 2 * piece + 1):
-                begin = (4 + i) * width
+            for i in range(runs[piece][0], sum(runs[piece])):
+                begin = (3 + i) * width
                 h = column_tile(k, begin)
                 deep = k * width
                 if deep:
@@ -406,8 +486,8 @@
     def update(c):
         span = slice(c * width, (c + 1) * width)
 
-        def tile(i, carry):
-            begin = pl.multiple_of((4 + i) * width, width)
+        def tile(i, spot):
+            begin = pl.multiple_of(spot * width, width)
             value = dot3(lower_of(begin, 4 * width), (uh[:, span], ul[:, span]))
             if c == 0:
                 at = pl.multiple_of(i * (2 * width), 8)
@@ -430,22 +510,27 @@
                 if c == 1:
                     part = mat[rows, :] - part
                 mat[rows, :] = part
+
+        def step(i, carry):
+            tile(i, 3 + i)
             return carry
 
-        lax.fori_loop(0, nrows, tile, 0)
-
-    def take(c, subtract, first, count):
+        tile(0, p)
+        lax.fori_loop(1, nrows, step, 0)
+
+    def take(c):
         def group(g, carry):
             for u in range(8):
-                row = taking[first + g * 8 + u]
-                value = full[c][pl.ds(row * 2, 2), :]
-                here = pl.ds((first + g * 8) * 6 + u * 6 + 2 * c, 2)
-                if subtract:
-                    value = value - mat[here, :]
-                mat[here, :] = value
+                row = table[TAKING + g * 8 + u]
+                here = pl.ds(g * 48 + u * 6 + 2 * c, 2)
+                mat[here, :] = full[c][pl.ds(row * 2, 2), :]
             return carry
 
-        lax.fori_loop(0, count // 8, group, 0)
+        lax.fori_loop(0, local_rows // 8, group, 0)
+
+    def leave(i):
+        rows = pl.ds(i * span6, span6)
+        return pltpu.make_async_copy(mat.at[rows], out.at[rows], mat_sem.at[i])
 
     for slot in range(3):
         pick_send(0, slot, 0)
@@ -462,12 +547,14 @@
     ih[...], il[...] = halves(inv[...])
     early_in(0)
     gather_start(0)
-    start(1, (0, 1, 2), 0)
+    start(1, (0, 1), 0)
+    start(1, (0, 1), 1)
     late_in(0)
-    pick(work, taking, 0, all0, 2, 0, local_rows)
+    pick(work, TAKING, all0, 2, 0, local_rows)
     column_start(0)
     gather_relay(0)
-    start(1, (0, 1, 2), 1)
+    start(1, (2,), 0)
+    start(1, (2,), 1)
     gather_end(0)
     column_start(3)
     column_start(4)
@@ -476,62 +563,59 @@
     column_pass(0)
     column_across(0)
     column_pass(3)
-    column_across(3)
     early_in(1)
     gather_start(1)
-    start(2, (0, 1, 2), 0)
+    start(2, (0, 1), 0)
     start(2, (0,), 1)
+    column_across(3)
     column_pass(4)
+    late_in(1)
+    take(1)
     column_across(4)
-    late_in(1)
-    take(1, False, 0, local_rows)
+    column_pass(1)
     gather_relay(1)
-    column_pass(1)
+    start(2, (2,), 0)
     column_ready(3)
     column_ready(4)
     corner()
-    column_across(1)
     column_pass(2)
     column_ready(0)
     panels(0)
+    column_across(1)
     column_across(2)
-    gather_end(1)
     column_ready(1)
     panels(1)
+    column_ready(2)
+    panels(2)
+    gather_end(1)
+    upper(0)
+    upper(1)
+    update(0)
     early_in(2)
     gather_start(2)
-    start(2, (1, 2), 1)
-    upper(0)
-    upper(1)
-    column_ready(2)
-    panels(2)
+    start(2, (1,), 1)
+    update(1)
     gather_relay(2)
-    update(0)
-    update(1)
+    start(2, (2,), 1)
     gather_end(2)
     upper(2)
     update(2)
+    for i in range(nrows):
+        leave(i).start()
+    mine_copy().wait()
     late_in(2)
-
-    def leave(i):
-        rows = pl.ds(i * span6, span6)
-        return pltpu.make_async_copy(mat.at[rows], out.at[rows], mat_sem.at[i])
-
-    for i in range(nrows):
-        take(2, True, i * width, width)
-        leave(i).start()
     for c in range(3):
         gather_sent(c)
         for slot in range(3):
             for part in range(2):
                 a2a(c, slot, part).wait_send()
-    for piece in range(5):
+    for piece in range(owned + 2):
         column_sent(piece)
     for i in range(nrows):
         leave(i).wait()
 
 
-def fused(matrix, sending, taking, heads, lower_fill, upper_fill, inverses, nrows, width):
+def fused(matrix, table, lower_fill, upper_fill, inverses, nrows, width):
     local_rows = nrows * width
     share = local_rows // 4
     dma = pltpu.SemaphoreType.DMA
@@ -539,42 +623,94 @@
     smem = pl.BlockSpec(memory_space=pltpu.SMEM)
     hbm = pl.BlockSpec(memory_space=pl.ANY)
     f32, bf16 = jnp.float32, jnp.bfloat16
-    rows = (4 + nrows) * width
+    tiles = 3 + nrows
     return pl.pallas_call(
         functools.partial(fused_kernel, nrows, width),
-        out_shape=jax.ShapeDtypeStruct((6 * local_rows, 128), f32),
-        in_specs=[smem] * 5 + [hbm, vmem],
-        out_specs=hbm,
+        out_shape=(
+            jax.ShapeDtypeStruct((6 * local_rows, 128), f32),
+            jax.ShapeDtypeStruct((2 * local_rows, 128), f32),
+        ),
+        in_specs=[smem] * 3 + [hbm, vmem],
+        out_specs=(hbm, hbm),
         scratch_shapes=[
             pltpu.VMEM((6 * local_rows, 128), f32),
             pltpu.VMEM((3, 3, 2 * share, 128), f32),
             *[pltpu.VMEM((8 * width, 128), f32)] * 3,
-            *[pltpu.VMEM((2 * local_rows, 128), f32)] * 3,
+            *[pltpu.VMEM((2 * local_rows, 128), f32)] * 2,
+            pltpu.VMEM((2 * (share - width), 128), f32),
             pltpu.VMEM((2 * local_rows, 128), f32),
             pltpu.VMEM((3, 8 * width, 128), f32),
-            pltpu.VMEM((4, 8 * width + 2 * local_rows, 128), f32),
-            *[pltpu.VMEM((rows, 4 * width), bf16)] * 2,
+            pltpu.VMEM((4, 2 * tiles * width, 128), f32),
+            *[pltpu.VMEM((tiles * width, 4 * width), bf16)] * 2,
             *[pltpu.VMEM((4 * width, 3 * width), bf16)] * 2,
             *[pltpu.VMEM((4, 3 * width, width), bf16)] * 2,
             *[pltpu.VMEM((4 * width, width), bf16)] * 2,
             dma((3, 3, 2)), dma((3, 3, 2)), dma((3, 4)), dma((3, 4)),
             dma((5,)), dma((5,)), dma((5,)), dma((5,)), dma((2, 5)), dma((2, 5)),
-            dma((5,)), dma((3, 4)), dma((7,)),
+            dma((5,)), dma((3, 4)), dma((8,)),
         ],
         compiler_params=pltpu.CompilerParams(
             collective_id=0, has_side_effects=True, vmem_limit_bytes=63 * 1024 * 1024
         ),
         name="fused",
-    )(sending, taking, heads, lower_fill, upper_fill, matrix, inverses.reshape(-1, width))
+    )(table, lower_fill, upper_fill, matrix, inverses.reshape(-1, width))
+
+
+def last_kernel(nrows, width, table, part, rows_in, out, mat, rows, sems):
+    span = 6 * width
+
+    def load(i):
+        here = pl.ds(i * span, span)
+        return pltpu.make_async_copy(part.at[here], mat.at[here], sems.at[0, i])
+
+    def store(i):
+        here = pl.ds(i * span, span)
+        return pltpu.make_async_copy(mat.at[here], out.at[here], sems.at[1, i])
+
+    incoming = pltpu.make_async_copy(rows_in, rows, sems.at[0, nrows])
+    incoming.start()
+    for i in range(nrows):
+        load(i).start()
+    incoming.wait()
+    for i in range(nrows):
+        load(i).wait()
+
+        def group(g, carry):
+            for u in range(8):
+                row = table[TAKING + i * width + g * 8 + u]
+                here = pl.ds(i * span + g * 48 + u * 6 + 4, 2)
+                mat[here, :] = rows[pl.ds(row * 2, 2), :] - mat[here, :]
+            return carry
+
+        lax.fori_loop(0, width // 8, group, 0)
+        store(i).start()
+    for i in range(nrows):
+        store(i).wait()
+
+
+def last(table, part, rows, nrows, width):
+    hbm = pl.BlockSpec(memory_space=pl.ANY)
+    return pl.pallas_call(
+        functools.partial(last_kernel, nrows, width),
+        out_shape=jax.ShapeDtypeStruct(part.shape, part.dtype),
+        in_specs=[pl.BlockSpec(memory_space=pltpu.SMEM), hbm, hbm],
+        out_specs=hbm,
+        scratch_shapes=[
+            pltpu.VMEM(part.shape, part.dtype),
+            pltpu.VMEM(rows.shape, rows.dtype),
+            pltpu.SemaphoreType.DMA((2, nrows + 1)),
+        ],
+        compiler_params=pltpu.CompilerParams(vmem_limit_bytes=60 * 1024 * 1024),
+        name="last",
+    )(table, part, rows)
 
 
 def kernel_body(matrix, row_order, inverses, lower_fill, upper_fill):
     nrows, width = matrix.shape[0], matrix.shape[2]
-    p = lax.axis_index("prow")
-    sending, taking, heads = tables(row_order, nrows, width, p)
+    table = tables(row_order, nrows, width)
     linear = matrix.reshape(nrows * width * 6, 128)
-    out = fused(linear, sending, taking, heads, lower_fill, upper_fill, inverses, nrows, width)
-    return out.reshape(matrix.shape)
+    part, rows = fused(linear, table, lower_fill, upper_fill, inverses, nrows, width)
+    return last(table, part, rows, nrows, width).reshape(matrix.shape)
 
 
 def solution(mesh):

time: 200 us -> 193 us (0.965)
  Pallas kernels: 181 us -> 193 us
  local copies, waits for them, and re-layouts: 10 us -> 0 us
  other arithmetic: 9.26 us -> 0 us
    pallas_call x1 -> x3, Pallas kernels: 181 us -> 193 us  [the longest x1 184 us: fused(): pl.pallas_call(functools.partial(fused_kernel, nrows, width), out_shape=(...]
    unnamed x2 -> x0, local copies, waits for them, and re-layouts: 7.78 us -> none
    sort x1 -> x0, other arithmetic: 5.6 us -> none  [tables(): both = lax.sort(both, is_stable=False)[:2 * local_rows] % local_rows]
    another operation x6 -> x0, other arithmetic: 2.83 us -> none
where the time goes in v2:
time: 193 us
  Pallas kernels  193 us (100%)
    pallas_call x1, Pallas kernels, fused(): pl.pallas_call(functools.partial(fused_kernel, nrows, width), out_shape=(...  184 us
    pallas_call x1, Pallas kernels, last(): pl.pallas_call(functools.partial(last_kernel, nrows, width), out_shape=ja...  6.42 us

profile of v2, /device:TPU:28, one launch (start us, length us, event | category | flops | bytes accessed | tf_op | source)
XLA Modules:
  0.0 193.2 jit_solution(12218257745442477140)
XLA Ops:
  0.0 2.6 %tables.1 = s32[40,128]{1,0:T(8,128)} custom-call(s32[48,128]{1,0:T(8,128)} %bitcast.9), custom_call_target="tpu_custom_call" | custom-call | tf_op jit(solution)/shard_map/tables/pallas_call | solution.py:180
  2.6 184.2 %fused.1 = (f32[9216,128]{1,0:T(8,128)}, f32[3072,128]{1,0:T(8,128)}) custom-call(s32[5120]{0:T(1024)} %bitcast.7, s32[4,24]{1,0:T(4,128)} %lower_fill.1, s32[4,24]{1,0:T(4,128)} %upper_fill.1, f32[9216,128]{1,0:T(8,128)} %bitcast.5, f32[1024,256]{1,0:T(8,128)} %bitcast.6), custom_call_target="tpu_custom_call" | custom-call | tf_op jit(solution)/shard_map/fused/pallas_call | solution.py:627
  186.8 6.4 %last.1 = f32[9216,128]{1,0:T(8,128)} custom-call(s32[5120]{0:T(1024)} %bitcast.8, f32[9216,128]{1,0:T(8,128)} %get-tuple-element.7.part, f32[3072,128]{1,0:T(8,128)} %get-tuple-element.8.rows_in), custom_call_target="tpu_custom_call" | custom-call | tf_op jit(solution)/shard_map/last/pallas_call | solution.py:693
